TPU v7x, 256 devices: a whole 4x4x8 slice. The times are simulated.
256 devices in a mesh: region: 128 (over z_hi, x, y, core), split: 2 (over z_lo).
Axes of the slice: x: 4, y: 4, z: 8 (z_hi: 4, z_lo: 2; z = z_hi * 2 + z_lo), core: 2. Of those that a mesh axis runs over, the one named last changes fastest.
Arguments:
- features: bfloat16 [96, 131072], P(None, ('region', 'split')), may hold values from -6 to 6
- kernel_one: bfloat16 [27, 96, 96], replicated, may hold values from -0.125 to 0.125
- kernel_two: bfloat16 [27, 96, 192], replicated, may hold values from -0.125 to 0.125
- occupancy: int32 [256, 512], P(('region', 'split')), may hold values 0 or 1
- neighbors: int32 [256, 27], P(('region', 'split')), may hold values from -1 to 255, as said below
- cotangent: bfloat16 [192, 131072], P(None, ('region', 'split')), may hold values from -0.016479492 to 0.016479492
Outputs:
- output: bfloat16 [192, 131072], P(None, ('region', 'split'))
- grad_one: float32 [27, 96, 96], replicated
- grad_two: float32 [27, 96, 192], replicated
Inputs may be any that keep to these rules, and one draw needn't show every extreme that they name: `neighbors`: entry k = 9 (dx + 1) + 3 (dy + 1) + (dz + 1) of a block's row is the active block whose block coordinates differ by (dx, dy, dz), or -1 if there is none; entry 13 is the block itself. Blocks are numbered in device order. The blocks of region r have x coordinate r and y coordinate 0 or 1; the device of split index s holds the blocks with z coordinate s. So a neighbour in region r - 1 or r + 1 differs by dx = -1 or +1, and a neighbour on the other device of the same region lies across the z boundary between the two halves.
All inputs are finite; a program needn't handle non-finite values. No bound on the sum of `occupancy` on one device may be relied on, other than what follows from the above.
Results may differ from a plain program's by a relative error of at most 0.0049.
Values may be sent and summed in bfloat16 or wider, within the bound.
A program may use at most 64 MiB of HBM per device.

v0:
```python
import jax
import jax.numpy as jnp
import numpy as np
from jax import lax
from jax.sharding import PartitionSpec as P


def padded(x, sides, width):
    for axis, dim in sides:
        count, length = (lax.axis_size(axis), x.shape[dim])
        up = [(i, (i + 1) % count) for i in range(count - 1)]
        down = [(j, i) for i, j in up]
        last = lax.slice_in_dim(x, length - width, length, axis=dim)
        first = lax.slice_in_dim(x, 0, width, axis=dim)
        before = lax.ppermute(last, axis, up)
        after = lax.ppermute(first, axis, down)
        x = jnp.concatenate([before, x, after], axis=dim)
    return x


def voxel_tables():
    voxels = np.arange(512)
    along_x = voxels // 64
    along_y = voxels // 8 % 8
    along_z = voxels % 8
    block_code = np.zeros((27, 512), np.int32)
    voxel_code = np.zeros((27, 512), np.int32)
    for offset in range(27):
        moved_x = along_x + offset // 9 - 1
        moved_y = along_y + offset // 3 % 3 - 1
        moved_z = along_z + offset % 3 - 1
        block_code[offset] = (moved_x // 8 + 1) * 9 + (moved_y // 8 + 1) * 3 + (moved_z // 8 + 1)
        voxel_code[offset] = moved_x % 8 * 64 + moved_y % 8 * 8 + moved_z % 8
    on_shell = (
        (along_x == 0)
        | (along_x == 7)
        | (along_y == 0)
        | (along_y == 7)
        | (along_z == 0)
        | (along_z == 7)
    )
    shell_voxels = voxels[on_shell].astype(np.int32)
    shell_slot = np.zeros(512, np.int32)
    shell_slot[shell_voxels] = np.arange(shell_voxels.shape[0], dtype=np.int32)
    return (block_code, voxel_code, shell_voxels, shell_slot)


def convolve(window_rows, lookup, kernel):

    def accumulate(offset, total):
        picked = jnp.take(
            window_rows, lax.dynamic_index_in_dim(lookup, offset, 0, keepdims=False), axis=0
        )
        weights = lax.dynamic_index_in_dim(kernel, offset, 0, keepdims=False)
        return total + jnp.dot(picked, weights, preferred_element_type=jnp.float32)

    return lax.fori_loop(
        0, 27, accumulate, jnp.zeros((lookup.shape[1], kernel.shape[2]), jnp.float32)
    )


def kernel_gradient(window_rows, lookup, gradient_rows):

    def accumulate(offset, total):
        picked = jnp.take(
            window_rows, lax.dynamic_index_in_dim(lookup, offset, 0, keepdims=False), axis=0
        )
        product = jnp.dot(picked.T, gradient_rows, preferred_element_type=jnp.float32)
        return lax.dynamic_update_index_in_dim(total, product, offset, 0)

    return lax.fori_loop(
        0,
        27,
        accumulate,
        jnp.zeros((27, window_rows.shape[1], gradient_rows.shape[1]), jnp.float32),
    )


def convolve_back(window_rows, lookup, kernel):

    def accumulate(offset, total):
        picked = jnp.take(
            window_rows, lax.dynamic_index_in_dim(lookup, 26 - offset, 0, keepdims=False), axis=0
        )
        weights = lax.dynamic_index_in_dim(kernel, offset, 0, keepdims=False)
        return total + jnp.dot(picked, weights.T, preferred_element_type=jnp.float32)

    return lax.fori_loop(
        0, 27, accumulate, jnp.zeros((lookup.shape[1], kernel.shape[1]), jnp.float32)
    )


def shards(features, kernel_one, kernel_two, occupancy, neighbors, cotangent):
    block_count = neighbors.shape[0]
    split_size = lax.axis_size("split")
    region_pos = lax.axis_index("region")
    window_first = (region_pos - 1) * split_size * block_count
    block_code, voxel_code, shell_voxels, shell_slot = voxel_tables()
    block_ids = jnp.transpose(jnp.take(neighbors, jnp.asarray(block_code), axis=1), (1, 0, 2))
    voxel_target = jnp.asarray(voxel_code)[:, None, :]
    window_cols = 3 * split_size * block_count * 512
    lookup = jnp.where(block_ids < 0, window_cols, (block_ids - window_first) * 512 + voxel_target)

    def spread(values):
        channels = values.shape[0]
        gathered = lax.all_gather(values, "split", axis=1, tiled=True)
        window = padded(gathered, (("region", 1),), gathered.shape[1])
        return jnp.concatenate([window, jnp.zeros((channels, 1), values.dtype)], axis=1).T

    lookup = lookup.reshape(27, -1).astype(jnp.int32)
    active = (occupancy.reshape(-1) > 0)[None, :]
    zero_value = jnp.zeros((), features.dtype)
    masked = jnp.where(active, features, zero_value)
    masked_window = spread(masked)
    hidden_pre = jnp.where(active, convolve(masked_window, lookup, kernel_one).T, 0.0)
    hidden = jnp.where(active, jax.nn.silu(hidden_pre), 0.0).astype(jnp.bfloat16)
    hidden_window = spread(hidden)
    output = jnp.where(active, convolve(hidden_window, lookup, kernel_two).T, 0.0)
    grad_out = jnp.where(active, cotangent, zero_value)
    grad_two = kernel_gradient(hidden_window, lookup, grad_out.T)
    back = convolve_back(spread(grad_out), lookup, kernel_two).T
    sigmoid_pre = jax.nn.sigmoid(hidden_pre)
    grad_pre = jnp.where(
        active, back * sigmoid_pre * (1.0 + hidden_pre * (1.0 - sigmoid_pre)), 0.0
    ).astype(jnp.bfloat16)
    grad_one = kernel_gradient(masked_window, lookup, grad_pre.T)
    grad_one, grad_two = lax.psum((grad_one, grad_two), ("region", "split"))
    return (output.astype(jnp.bfloat16), grad_one, grad_two)


def solution(mesh):
    in_specs = (
        P(None, ("region", "split")),
        P(),
        P(),
        P(("region", "split"), None),
        P(("region", "split"), None),
        P(None, ("region", "split")),
    )
    out_specs = (P(None, ("region", "split")), P(), P())
    return jax.shard_map(shards, mesh=mesh, in_specs=in_specs, out_specs=out_specs, check_vma=False)
```

profile of v0, /device:TPU:2, one launch (start us, length us, event | category | flops | bytes accessed | tf_op | source)
XLA Modules:
  0.0 733.8 jit_solution(8820615939577342043)
XLA Ops:
  8.8 5.4 all_gather.9
  14.2 3.6 collective-permute-start.1
  21.0 8.9 %all_gather.11 = bf16[192,1024]{0,1:T(8,128)(2,1)S(1)} all-gather(bf16[192,512]{0,1:T(8,128)(2,1)S(1)} %broadcast_select_fusion), channel_id=1, replica_groups=mesh['region'=128,'split'=2] {'split'}, dimensions={1}, use_global_device_ids=true | all-gather | bytes 589824 | tf_op jit(solution)/shard_map/all_gather | solution.py:106
  29.9 4.0 collective-permute-start.5
  35.9 77.0 %gather_fusion.5 = s32[13824]{0:T(1024)S(1)} fusion(s32[27]{0:T(128)S(1)} %bitcast.83, s32[14336]{0:T(1024)S(1)} %pad_clamp_fusion.5), kind=kCustom, calls=%fused_computation.5 | custom fusion | bytes 165888 | tf_op jit(solution)/shard_map/jit(_take)/gather | solution.py:99
  113.6 67.2 %while.72 = (s32[]{:T(128)}, f32[512,96]{0,1:T(8,128)S(1)}, s32[27,512]{1,0:T(8,128)S(1)}, bf16[3073,96]{1,0:T(8,128)(2,1)S(1)}, bf16[27,96,96]{2,1,0:T(8,128)(2,1)}, /*index=5*/s32[]{:T(128)}, s32[]{:T(128)}) while((s32[]{:T(128)}, f32[512,96]{0,1:T(8,128)S(1)}, s32[27,512]{1,0:T(8,128)S(1)}, bf16[3073,96]{1,0:T(8,128)(2,1)S(1)}, ...), condition=%wide.region_1.3_spmd.clone, body=%wide.region_0.0_spmd.clone.sunk | while | flops 9590275 | bytes 732263 | solution.py:57
  180.8 5.3 all_gather.10
  186.1 4.7 collective-permute-start.3
  194.0 5.9 collective-permute-done.2
  203.1 106.1 %while.74 = (s32[]{:T(128)}, f32[512,96]{0,1:T(8,128)}, s32[27,512]{1,0:T(8,128)S(1)}, bf16[3073,192]{1,0:T(8,128)(2,1)S(1)}, bf16[27,96,192]{2,1,0:T(8,128)(2,1...) while((s32[]{:T(128)}, f32[512,96]{0,1:T(8,128)}, s32[27,512]{1,0:T(8,128)S(1)}, ...), condition=%wide.region_5.7_spmd.clone, body=%wide.region_4.6_spmd.clone.sunk | while | flops 19076616 | bytes 1049765 | solution.py:88
  203.2 2.0 gather_fusion.4
  206.9 2.0 gather_fusion.4
  210.9 2.0 gather_fusion.4
  214.8 2.0 gather_fusion.4
  216.8 1.9 convolution_add_fusion.8
  218.7 2.0 gather_fusion.4
  222.7 2.0 gather_fusion.4
  226.6 2.0 gather_fusion.4
  230.5 2.0 gather_fusion.4
  232.5 1.9 convolution_add_fusion.8
  234.5 2.0 gather_fusion.4
  238.4 2.0 gather_fusion.4
  240.4 1.9 convolution_add_fusion.8
  242.3 2.0 gather_fusion.4
  244.3 1.9 convolution_add_fusion.8
  246.3 2.0 gather_fusion.4
  250.2 2.0 gather_fusion.4
  254.2 2.0 gather_fusion.4
  256.1 1.9 convolution_add_fusion.8
  258.1 2.0 gather_fusion.4
  260.0 1.9 convolution_add_fusion.8
  262.0 2.0 gather_fusion.4
  266.0 2.0 gather_fusion.4
  269.9 2.0 gather_fusion.4
  273.8 2.0 gather_fusion.4
  277.8 2.0 gather_fusion.4
  281.7 2.0 gather_fusion.4
  285.6 2.0 gather_fusion.4
  289.6 2.0 gather_fusion.4
  293.5 2.0 gather_fusion.4
  297.4 2.0 gather_fusion.4
  301.4 2.0 gather_fusion.4
  305.3 2.0 gather_fusion.4
  310.5 63.1 %while.70 = (s32[]{:T(128)}, f32[27,96,96]{2,1,0:T(8,128)}, s32[27,512]{1,0:T(8,128)S(1)}, bf16[3073,96]{1,0:T(8,128)(2,1)S(1)}, bf16[512,96]{1,0:T(8,128)(2,1)S(1)}, /*index=5*/s32[]{:T(128)}) while((s32[]{:T(128)}, f32[27,96,96]{2,1,0:T(8,128)}, s32[27,512]{1,0:T(8,128)S(1)}, bf16[3073,96]{1,0:T(8,128)(2,1)S(1)}, ...), condition=%wide.region_7.9_spmd, body=%wide.region_6.8_spmd.sunk | while | flops 9491970 | bytes 461909 | solution.py:71
  373.6 63.7 %while.71 = (s32[]{:T(128)}, f32[27,96,192]{2,1,0:T(8,128)}, s32[27,512]{1,0:T(8,128)S(1)}, bf16[3073,96]{1,0:T(8,128)(2,1)S(1)}, bf16[512,192]{1,0:T(8,128)(2,1)S(1)}, /*index=5*/s32[]{:T(128)}) while((s32[]{:T(128)}, f32[27,96,192]{2,1,0:T(8,128)}, s32[27,512]{1,0:T(8,128)S(1)}, bf16[3073,96]{1,0:T(8,128)(2,1)S(1)}, ...), condition=%wide.region_10.12_spmd, body=%wide.region_9.11_spmd.sunk | while | flops 18929152 | bytes 609365 | solution.py:71
  438.3 69.8 %while.73 = (s32[]{:T(128)}, f32[512,192]{0,1:T(8,128)S(1)}, s32[27,512]{1,0:T(8,128)S(1)}, bf16[3073,96]{1,0:T(8,128)(2,1)S(1)}, bf16[27,96,192]{2,1,0:T(8,128)(2,1)}, /*index=5*/s32[]{:T(128)}, s32[]{:T(128)}) while((s32[]{:T(128)}, f32[512,192]{0,1:T(8,128)S(1)}, s32[27,512]{1,0:T(8,128)S(1)}, bf16[3073,96]{1,0:T(8,128)(2,1)S(1)}, ...), condition=%wide.region_3.5_spmd.clone, body=%wide.region_2.4_spmd.clone.sunk | while | flops 19125764 | bytes 1150055 | solution.py:57
  508.8 214.0 %all-reduce.3.cloned.1.call-done = (f32[27,96,96]{2,1,0:T(8,128)}, f32[27,96,192]{2,1,0:T(8,128)}) async-done(((f32[27,96,96]{2,1,0:T(8,128)}, f32[27,96,192]{2,1,0:T(8,128)}), (f32[27,96,96]{2,1,0:T(8,128)}, f32[27,96,192]{2,1,0:T(8,128)})) %all-reduce.3.cloned.1.call-update) | async-done | bytes 2986000 | tf_op jit(solution)/shard_map/psum | solution.py:127
  722.9 2.6 copy.57
  (802 shorter events, 318.3 us)
Async XLA Ops:
  7.2 28.7 %copy-start = (s32[1,27]{1,0:T(1,128)S(1)}, s32[1,27]{1,0:T(1,128)}, u32[]{:S(2)}) copy-start(s32[1,27]{1,0:T(1,128)} %param.24) | copy-start | bytes 328
  7.2 28.7 %copy-start.7 = (s32[13824]{0:T(1024)S(1)}, s32[13824]{0:T(1024)}, u32[]{:S(2)}) copy-start(s32[13824]{0:T(1024)} %constant.268) | copy-start | bytes 165892
  7.2 715.7 %all-reduce.3.cloned.1.call-start = ((), (), s32[]{:S(2)}) async-start(), calls=%async_computation | async-start | bytes 7962624 | tf_op jit(solution)/shard_map/psum | solution.py:127
  14.2 98.8 %collective-permute-start.1 = (bf16[96,1024]{1,0:T(8,128)(2,1)S(1)}, bf16[96,1024]{1,0:T(8,128)(2,1)S(1)}, u32[]{:S(2)}, u32[]{:S(2)}) collective-permute-start(bf16[96,1024]{1,0:T(8,128)(2,1)S(1)} %all_gather.9), channel_id=1, source_target_pairs={{2,0},{4,2},{6,4},{8,6},{10,8},{12,10},{14,12},{16,14},{18,16},{20... | collective-permute-start | bytes 589832 | tf_op jit(solution)/shard_map/ppermute | solution.py:16
  17.9 95.2 %collective-permute-start = (bf16[96,1024]{1,0:T(8,128)(2,1)S(1)}, bf16[96,1024]{1,0:T(8,128)(2,1)S(1)}, u32[]{:S(2)}, u32[]{:S(2)}) collective-permute-start(bf16[96,1024]{1,0:T(8,128)(2,1)S(1)} %all_gather.9), channel_id=1, source_target_pairs={{0,2},{2,4},{4,6},{6,8},{8,10},{10,12},{12,14},{14,16},{16,18},{18... | collective-permute-start | bytes 589832 | tf_op jit(solution)/shard_map/ppermute | solution.py:15
  29.9 83.0 %copy-start.5 = (bf16[192,1024]{0,1:T(8,128)(2,1)}, bf16[192,1024]{0,1:T(8,128)(2,1)S(1)}, u32[]{:S(2)}) copy-start(bf16[192,1024]{0,1:T(8,128)(2,1)S(1)} %all_gather.11) | copy-start | bytes 1179652
  29.9 170.5 %collective-permute-start.5 = (bf16[192,1024]{0,1:T(8,128)(2,1)S(1)}, bf16[192,1024]{0,1:T(8,128)(2,1)S(1)}, u32[]{:S(2)}, u32[]{:S(2)}) collective-permute-start(bf16[192,1024]{0,1:T(8,128)(2,1)S(1)} %all_gather.11), channel_id=1, source_target_pairs={{2,0},{4,2},{6,4},{8,6},{10,8},{12,10},{14,12},{16,14},{18,16},{20... | collective-permute-start | bytes 1179656 | tf_op jit(solution)/shard_map/ppermute | solution.py:16
  33.9 167.3 %collective-permute-start.4 = (bf16[192,1024]{0,1:T(8,128)(2,1)S(1)}, bf16[192,1024]{0,1:T(8,128)(2,1)}, u32[]{:S(2)}, u32[]{:S(2)}) collective-permute-start(bf16[192,1024]{0,1:T(8,128)(2,1)S(1)} %all_gather.11), channel_id=1, source_target_pairs={{0,2},{2,4},{4,6},{6,8},{8,10},{10,12},{12,14},{14,16},{16,18},{18... | collective-permute-start | bytes 1179656 | tf_op jit(solution)/shard_map/ppermute | solution.py:15
  35.9 77.0 %copy-start.8 = (s32[13824]{0:T(1024)S(1)}, s32[13824]{0:T(1024)}, u32[]{:S(2)}) copy-start(s32[13824]{0:T(1024)} %constant.270) | copy-start | bytes 165892
  180.8 19.1 %copy-start.2 = (f32[512,96]{0,1:T(8,128)}, f32[512,96]{0,1:T(8,128)S(1)}, u32[]{:S(2)}) copy-start(f32[512,96]{0,1:T(8,128)S(1)} %get-tuple-element.512) | copy-start | bytes 589828
  186.1 7.8 %collective-permute-start.3 = (bf16[96,1024]{1,0:T(8,128)(2,1)S(1)}, bf16[96,1024]{1,0:T(8,128)(2,1)S(1)}, u32[]{:S(2)}, u32[]{:S(2)}) collective-permute-start(bf16[96,1024]{1,0:T(8,128)(2,1)S(1)} %all_gather.10), channel_id=1, source_target_pairs={{2,0},{4,2},{6,4},{8,6},{10,8},{12,10},{14,12},{16,14},{18,16},{20... | collective-permute-start | bytes 589832 | tf_op jit(solution)/shard_map/ppermute | solution.py:16
  190.8 9.1 %collective-permute-start.2 = (bf16[96,1024]{1,0:T(8,128)(2,1)S(1)}, bf16[96,1024]{1,0:T(8,128)(2,1)S(1)}, u32[]{:S(2)}, u32[]{:S(2)}) collective-permute-start(bf16[96,1024]{1,0:T(8,128)(2,1)S(1)} %all_gather.10), channel_id=1, source_target_pairs={{0,2},{2,4},{4,6},{6,8},{8,10},{10,12},{12,14},{14,16},{16,18},{18... | collective-permute-start | bytes 589832 | tf_op jit(solution)/shard_map/ppermute | solution.py:15
  200.4 0.8 copy-start.6
  310.4 63.2 %copy-start.3 = (bf16[512,192]{1,0:T(8,128)(2,1)S(1)}, bf16[512,192]{1,0:T(8,128)(2,1)}, u32[]{:S(2)}) copy-start(bf16[512,192]{1,0:T(8,128)(2,1)} %fusion.39) | copy-start | bytes 589828
  437.3 1.0 copy-start.1
  722.9 2.6 copy-start.4
Sparse Core Ops, SparseCore 0:
  437.4 285.4 all-reduce.2
where the time goes:
time: 738 us; the launch traced here: 734 us
  local copies, waits for them, and re-layouts  283 us (38%)
  waiting for transfers between devices  220 us (30%)
  matrix products  164 us (22%)
  blocking collectives  19.6 us (3%)
  starting transfers between devices  18.1 us (2%)
  between operations  14.4 us (2%)
  other arithmetic  9.17 us (1%)
    psum x1, waiting for transfers between devices, shards(): grad_one, grad_two = lax.psum((grad_one, grad_two), ('region', 'split'))  214 us
    gather x108, local copies, waits for them, and re-layouts, accumulate(): jnp.take(window_rows, lax.dynamic_index_in_dim(lookup, offset, 0, keepdim...  145 us
    gather x1, local copies, waits for them, and re-layouts, shards(): jnp.take(neighbors, jnp.asarray(block_code), axis=1)  77 us
    dot_general x54, matrix products, accumulate(): return total + jnp.dot(picked, weights, preferred_element_type=jnp.float32)  59.8 us
    gather x27, local copies, waits for them, and re-layouts, accumulate(): jnp.take(window_rows, lax.dynamic_index_in_dim(lookup, 26 - offset, 0, ke...  52.7 us
    dot_general x27, matrix products, accumulate(): jnp.dot(picked, weights.T, preferred_element_type=jnp.float32)  52.1 us
    dot_general x54, matrix products, accumulate(): jnp.dot(picked.T, gradient_rows, preferred_element_type=jnp.float32)  51.7 us
    all_gather x3, blocking collectives, spread(): gathered = lax.all_gather(values, 'split', axis=1, tiled=True)  19.6 us
  transfers between devices with their start and end apart: 7, of which 3 were waited for; matrix products, arithmetic and copies ran while one was open for 29% of the time, Pallas kernels for 0%

commit v1 on v0

--- a/solution.py
+++ b/solution.py
@@ -3,6 +3,10 @@
 import numpy as np
 from jax import lax
 from jax.sharding import PartitionSpec as P
+
+scan_rings = lambda slab_in, peer_axis, axis_id: lax.psum(
+    lax.psum(slab_in, axis_name=peer_axis), axis_name=axis_id
+)
 
 
 def padded(x, sides, width):
@@ -124,7 +128,7 @@
         active, back * sigmoid_pre * (1.0 + hidden_pre * (1.0 - sigmoid_pre)), 0.0
     ).astype(jnp.bfloat16)
     grad_one = kernel_gradient(masked_window, lookup, grad_pre.T)
-    grad_one, grad_two = lax.psum((grad_one, grad_two), ("region", "split"))
+    grad_one, grad_two = scan_rings((grad_one, grad_two), "split", "region")
     return (output.astype(jnp.bfloat16), grad_one, grad_two)
 
 

time: 738 us -> 1940 us (2.63); the launches traced: 734 us -> 1910 us
  waiting for transfers between devices: 220 us -> 1400 us
    psum x1 -> x2, waiting for transfers between devices: 214 us -> 1390 us  [the longest x1 1270 us: lax.psum(lax.psum(slab_in, axis_name=peer_axis), axis_name=axis_id)]
  transfers between devices with their start and end apart: 7 -> 8, of which waited for: 3 -> 4; matrix products, arithmetic and copies ran while one was open for 29% -> 11% of each run, Pallas kernels for 0% -> 0%
where the time goes in v1:
time: 1940 us; the launch traced here: 1910 us
  waiting for transfers between devices  1400 us (72%)
  local copies, waits for them, and re-layouts  282 us (15%)
  matrix products  164 us (8%)
  blocking collectives  19.6 us (1%)
    psum x1, waiting for transfers between devices, lax.psum(lax.psum(slab_in, axis_name=peer_axis), axis_name=axis_id)  1270 us
    gather x108, local copies, waits for them, and re-layouts, accumulate(): jnp.take(window_rows, lax.dynamic_index_in_dim(lookup, offset, 0, keepdim...  145 us
    psum x1, waiting for transfers between devices, lax.psum(slab_in, axis_name=peer_axis)  129 us
    gather x1, local copies, waits for them, and re-layouts, shards(): jnp.take(neighbors, jnp.asarray(block_code), axis=1)  77 us
    dot_general x54, matrix products, accumulate(): return total + jnp.dot(picked, weights, preferred_element_type=jnp.float32)  59.8 us
    gather x27, local copies, waits for them, and re-layouts, accumulate(): jnp.take(window_rows, lax.dynamic_index_in_dim(lookup, 26 - offset, 0, ke...  52.7 us
    dot_general x27, matrix products, accumulate(): jnp.dot(picked, weights.T, preferred_element_type=jnp.float32)  52.1 us
    dot_general x54, matrix products, accumulate(): jnp.dot(picked.T, gradient_rows, preferred_element_type=jnp.float32)  51.7 us
  transfers between devices with their start and end apart: 8, of which 4 were waited for; matrix products, arithmetic and copies ran while one was open for 11% of the time, Pallas kernels for 0%

profile of v1, /device:TPU:2, one launch (start us, length us, event | category | flops | bytes accessed | tf_op | source)
XLA Modules:
  0.0 1913.6 jit_solution(3622494542035522460)
XLA Ops:
  8.8 5.4 all_gather.9
  14.2 3.6 collective-permute-start.1
  21.0 8.9 all_gather.11
  29.9 4.0 collective-permute-start.5
  35.9 77.0 %gather_fusion.5 = s32[13824]{0:T(1024)S(1)} fusion(s32[27]{0:T(128)S(1)} %bitcast.83, s32[14336]{0:T(1024)S(1)} %pad_clamp_fusion.5), kind=kCustom, calls=%fused_computation.5 | custom fusion | bytes 165888 | tf_op jit(solution)/shard_map/jit(_take)/gather | solution.py:103
  113.6 67.1 %while.72 = (s32[]{:T(128)}, f32[512,96]{0,1:T(8,128)S(1)}, s32[27,512]{1,0:T(8,128)S(1)}, bf16[3073,96]{1,0:T(8,128)(2,1)S(1)}, bf16[27,96,96]{2,1,0:T(8,128)(2,1)}, /*index=5*/s32[]{:T(128)}, s32[]{:T(128)}) while((s32[]{:T(128)}, f32[512,96]{0,1:T(8,128)S(1)}, s32[27,512]{1,0:T(8,128)S(1)}, bf16[3073,96]{1,0:T(8,128)(2,1)S(1)}, ...), condition=%wide.region_1.3_spmd.clone, body=%wide.region_0.0_spmd.clone.sunk | while | flops 9590275 | bytes 732263 | solution.py:61
  180.8 5.3 all_gather.10
  186.0 4.7 collective-permute-start.3
  193.9 5.9 collective-permute-done.2
  203.0 106.1 %while.74 = (s32[]{:T(128)}, f32[512,96]{0,1:T(8,128)}, s32[27,512]{1,0:T(8,128)S(1)}, bf16[3073,192]{1,0:T(8,128)(2,1)S(1)}, bf16[27,96,192]{2,1,0:T(8,128)(2,1...) while((s32[]{:T(128)}, f32[512,96]{0,1:T(8,128)}, s32[27,512]{1,0:T(8,128)S(1)}, ...), condition=%wide.region_5.7_spmd.clone, body=%wide.region_4.6_spmd.clone.sunk | while | flops 19076616 | bytes 1049765 | solution.py:92
  203.1 2.0 gather_fusion.4
  206.9 2.0 gather_fusion.4
  208.9 1.9 convolution_add_fusion.8
  210.8 2.0 gather_fusion.4
  214.8 2.0 gather_fusion.4
  216.7 1.9 convolution_add_fusion.8
  218.7 2.0 gather_fusion.4
  220.7 1.9 convolution_add_fusion.8
  222.6 2.0 gather_fusion.4
  226.6 2.0 gather_fusion.4
  230.5 2.0 gather_fusion.4
  232.5 1.9 convolution_add_fusion.8
  234.4 2.0 gather_fusion.4
  236.4 1.9 convolution_add_fusion.8
  238.4 2.0 gather_fusion.4
  242.3 2.0 gather_fusion.4
  246.2 2.0 gather_fusion.4
  250.2 2.0 gather_fusion.4
  254.1 2.0 gather_fusion.4
  258.1 2.0 gather_fusion.4
  262.0 2.0 gather_fusion.4
  265.9 2.0 gather_fusion.4
  269.9 2.0 gather_fusion.4
  273.8 2.0 gather_fusion.4
  277.7 2.0 gather_fusion.4
  281.7 2.0 gather_fusion.4
  285.6 2.0 gather_fusion.4
  289.5 2.0 gather_fusion.4
  293.5 2.0 gather_fusion.4
  297.4 2.0 gather_fusion.4
  301.3 2.0 gather_fusion.4
  305.3 2.0 gather_fusion.4
  310.4 63.1 %while.70 = (s32[]{:T(128)}, f32[27,96,96]{2,1,0:T(8,128)}, s32[27,512]{1,0:T(8,128)S(1)}, bf16[3073,96]{1,0:T(8,128)(2,1)S(1)}, bf16[512,96]{1,0:T(8,128)(2,1)S(1)}, /*index=5*/s32[]{:T(128)}) while((s32[]{:T(128)}, f32[27,96,96]{2,1,0:T(8,128)}, s32[27,512]{1,0:T(8,128)S(1)}, bf16[3073,96]{1,0:T(8,128)(2,1)S(1)}, ...), condition=%wide.region_7.9_spmd, body=%wide.region_6.8_spmd.sunk | while | flops 9491970 | bytes 461909 | solution.py:75
  373.5 63.6 %while.71 = (s32[]{:T(128)}, f32[27,96,192]{2,1,0:T(8,128)}, s32[27,512]{1,0:T(8,128)S(1)}, bf16[3073,96]{1,0:T(8,128)(2,1)S(1)}, bf16[512,192]{1,0:T(8,128)(2,1)S(1)}, /*index=5*/s32[]{:T(128)}) while((s32[]{:T(128)}, f32[27,96,192]{2,1,0:T(8,128)}, s32[27,512]{1,0:T(8,128)S(1)}, bf16[3073,96]{1,0:T(8,128)(2,1)S(1)}, ...), condition=%wide.region_11.13_spmd, body=%wide.region_10.12_spmd.sunk | while | flops 18929152 | bytes 609365 | solution.py:75
  437.2 128.9 %all-reduce.7.cloned.1.call-done = (f32[27,96,96]{2,1,0:T(8,128)}, f32[27,96,192]{2,1,0:T(8,128)}) async-done(((f32[27,96,96]{2,1,0:T(8,128)}, f32[27,96,192]{2,1,0:T(8,128)}), (f32[27,96,96]{2,1,0:T(8,128)}, f32[27,96,192]{2,1,0:T(8,128)})) %all-reduce.7.cloned.1.call-update) | async-done | bytes 2986000 | tf_op jit(solution)/shard_map/psum | solution.py:8
  566.2 69.9 %while.73 = (s32[]{:T(128)}, f32[512,192]{0,1:T(8,128)S(1)}, s32[27,512]{1,0:T(8,128)S(1)}, bf16[3073,96]{1,0:T(8,128)(2,1)S(1)}, bf16[27,96,192]{2,1,0:T(8,128)(2,1)}, /*index=5*/s32[]{:T(128)}, s32[]{:T(128)}) while((s32[]{:T(128)}, f32[512,192]{0,1:T(8,128)S(1)}, s32[27,512]{1,0:T(8,128)S(1)}, bf16[3073,96]{1,0:T(8,128)(2,1)S(1)}, ...), condition=%wide.region_3.5_spmd.clone, body=%wide.region_2.4_spmd.clone.sunk | while | flops 19125764 | bytes 1150055 | solution.py:61
  636.8 1265.8 %all-reduce.5.cloned.1.call-done = (f32[27,96,96]{2,1,0:T(8,128)}, f32[27,96,192]{2,1,0:T(8,128)}) async-done(((f32[27,96,96]{2,1,0:T(8,128)}, f32[27,96,192]{2,1,0:T(8,128)}), (f32[27,96,96]{2,1,0:T(8,128)}, f32[27,96,192]{2,1,0:T(8,128)})) %all-reduce.5.cloned.1.call-update) | async-done | bytes 2986000 | tf_op jit(solution)/shard_map/psum | solution.py:7
  1902.6 2.6 copy.59
  (803 shorter events, 319.2 us)
Async XLA Ops:
  7.2 28.7 %copy-start = (s32[1,27]{1,0:T(1,128)S(1)}, s32[1,27]{1,0:T(1,128)}, u32[]{:S(2)}) copy-start(s32[1,27]{1,0:T(1,128)} %param.24) | copy-start | bytes 328
  7.2 28.7 %copy-start.6 = (s32[13824]{0:T(1024)S(1)}, s32[13824]{0:T(1024)}, u32[]{:S(2)}) copy-start(s32[13824]{0:T(1024)} %constant.268) | copy-start | bytes 165892
  7.2 559.0 %all-reduce.7.cloned.1.call-start = ((), (), s32[]{:S(2)}) async-start(), calls=%async_computation.1 | async-start | bytes 7962624 | tf_op jit(solution)/shard_map/psum | solution.py:8
  14.2 98.8 %collective-permute-start.1 = (bf16[96,1024]{1,0:T(8,128)(2,1)S(1)}, bf16[96,1024]{1,0:T(8,128)(2,1)S(1)}, u32[]{:S(2)}, u32[]{:S(2)}) collective-permute-start(bf16[96,1024]{1,0:T(8,128)(2,1)S(1)} %all_gather.9), channel_id=1, source_target_pairs={{2,0},{4,2},{6,4},{8,6},{10,8},{12,10},{14,12},{16,14},{18,16},{20... | collective-permute-start | bytes 589832 | tf_op jit(solution)/shard_map/ppermute | solution.py:20
  17.9 95.2 %collective-permute-start = (bf16[96,1024]{1,0:T(8,128)(2,1)S(1)}, bf16[96,1024]{1,0:T(8,128)(2,1)S(1)}, u32[]{:S(2)}, u32[]{:S(2)}) collective-permute-start(bf16[96,1024]{1,0:T(8,128)(2,1)S(1)} %all_gather.9), channel_id=1, source_target_pairs={{0,2},{2,4},{4,6},{6,8},{8,10},{10,12},{12,14},{14,16},{16,18},{18... | collective-permute-start | bytes 589832 | tf_op jit(solution)/shard_map/ppermute | solution.py:19
  29.9 83.0 %copy-start.4 = (bf16[192,1024]{0,1:T(8,128)(2,1)}, bf16[192,1024]{0,1:T(8,128)(2,1)S(1)}, u32[]{:S(2)}) copy-start(bf16[192,1024]{0,1:T(8,128)(2,1)S(1)} %all_gather.11) | copy-start | bytes 1179652
  29.9 170.5 %collective-permute-start.5 = (bf16[192,1024]{0,1:T(8,128)(2,1)S(1)}, bf16[192,1024]{0,1:T(8,128)(2,1)S(1)}, u32[]{:S(2)}, u32[]{:S(2)}) collective-permute-start(bf16[192,1024]{0,1:T(8,128)(2,1)S(1)} %all_gather.11), channel_id=1, source_target_pairs={{2,0},{4,2},{6,4},{8,6},{10,8},{12,10},{14,12},{16,14},{18,16},{20... | collective-permute-start | bytes 1179656 | tf_op jit(solution)/shard_map/ppermute | solution.py:20
  33.9 167.3 %collective-permute-start.4 = (bf16[192,1024]{0,1:T(8,128)(2,1)S(1)}, bf16[192,1024]{0,1:T(8,128)(2,1)}, u32[]{:S(2)}, u32[]{:S(2)}) collective-permute-start(bf16[192,1024]{0,1:T(8,128)(2,1)S(1)} %all_gather.11), channel_id=1, source_target_pairs={{0,2},{2,4},{4,6},{6,8},{8,10},{10,12},{12,14},{14,16},{16,18},{18... | collective-permute-start | bytes 1179656 | tf_op jit(solution)/shard_map/ppermute | solution.py:19
  35.9 77.0 %copy-start.7 = (s32[13824]{0:T(1024)S(1)}, s32[13824]{0:T(1024)}, u32[]{:S(2)}) copy-start(s32[13824]{0:T(1024)} %constant.270) | copy-start | bytes 165892
  180.7 19.2 %copy-start.1 = (f32[512,96]{0,1:T(8,128)}, f32[512,96]{0,1:T(8,128)S(1)}, u32[]{:S(2)}) copy-start(f32[512,96]{0,1:T(8,128)S(1)} %get-tuple-element.512) | copy-start | bytes 589828
  186.0 7.8 collective-permute-start.3
  190.7 9.1 collective-permute-start.2
  200.4 0.8 copy-start.5
  310.4 63.1 %copy-start.2 = (bf16[512,192]{1,0:T(8,128)(2,1)S(1)}, bf16[512,192]{1,0:T(8,128)(2,1)}, u32[]{:S(2)}) copy-start(bf16[512,192]{1,0:T(8,128)(2,1)} %fusion.39) | copy-start | bytes 589828
  437.2 1465.4 %all-reduce.5.cloned.1.call-start = ((), (), s32[]{:S(2)}) async-start(), calls=%async_computation | async-start | bytes 7962624 | tf_op jit(solution)/shard_map/psum | solution.py:7
  1902.6 2.6 copy-start.3
Sparse Core Ops, SparseCore 0:
  437.3 128.8 all-reduce.6
  568.9 1333.6 all-reduce.4
